TPU v7x, 32 devices: a whole 2x2x4 slice. The times are simulated.
32 devices in a mesh: atom: 8 (over z, x), aux: 4 (over y, core).
Axes of the slice: x: 2, y: 2, z: 4, core: 2. Of those that a mesh axis runs over, the one named last changes fastest.
Arguments:
- three_index: bfloat16 [128, 32, 128, 128], P('atom', 'aux'), may hold values from -6 to 6
- pair_mask: int32 [128, 8, 8], P('atom'), may hold values 0 or 1
- pair_owner: int32 [128, 1], P('atom'), may hold values from 0 to 7; in each aligned block of 16 rows (0 to 15, 16 to 31, ...) at most 2 rows name the same one
- pair_sub: int32 [128], P('atom'), may hold values from 0 to 3
- pair_nu: int32 [128], P('atom'), may hold values from 0 to 31
- live_count: int32 [8], P('atom'), may hold values from 1 to 16, 96 in all
- coefficients: bfloat16 [4096, 128], P('atom'), may hold values from -0.5 to 0.5
- fit_matrix: bfloat16 [32, 32], P('aux'), as said below
Outputs:
- exchange: float32 [4096, 4096], P('atom', 'aux')
Inputs may be any that keep to these rules, and one draw needn't show every extreme that they name: `pair_owner`: among the 16 slots of one atom index, at most 2 name the same owner, and in every draw some owner is named exactly 2 times by some atom index's slots. The first live_count[a] slots of atom index a are live; some atom index has all 16 slots live. `fit_matrix`: Symmetric.
All inputs are finite; a program needn't handle non-finite values. No bound on the sum of `pair_mask` or of `live_count` on one device may be relied on, other than what follows from the above.
Results may differ from a plain program's by a relative error of at most 0.012.
Values may be sent and summed in bfloat16 or wider, within the bound.
A program may use at most 128 MiB of HBM per device.

v0:
```python
import functools

import jax
import jax.numpy as jnp
from jax import lax
from jax.experimental import pallas as pl
from jax.experimental.pallas import tpu as pltpu
from jax.sharding import PartitionSpec as P

CAP = 2
MESH = pl.DeviceIdType.MESH


def exchange_kernel(
    atoms, auxes, h_ref, fit_ref, out_ref,
    hall, hx, g, epart, cbuf, ybuf,
    local_sem, sx, sz0, sz, rh, sa, ra, sc, rc, sy, ry,
):
    planes, ys = atoms // 2, auxes // 2
    aux_here, rows, occ = h_ref.shape
    me = lax.axis_index("atom")
    ax = lax.axis_index("aux")
    hi, lo = me // 2, me % 2
    y, c = ax // 2, ax % 2
    partner = {"atom": hi * 2 + 1 - lo, "aux": ax}
    peer = {"atom": me, "aux": y * 2 + 1 - c}

    barrier = pltpu.get_barrier_semaphore()

    def greet(device):
        pl.semaphore_signal(barrier, inc=1, device_id=device, device_id_type=MESH)

    greet(partner)
    greet(peer)
    for d in range(1, ys):
        greet({"atom": me, "aux": ((y + d) % ys) * 2 + c})

    @pl.when(hi > 0)
    def _():
        greet({"atom": me - 2, "aux": ax})

    @pl.when(hi < planes - 1)
    def _():
        greet({"atom": me + 2, "aux": ax})

    before = jnp.minimum(hi, 1)
    behind = jnp.minimum(planes - 1 - hi, 1)
    pl.semaphore_wait(barrier, 1 + ys + before + behind)

    def remote(src, dst, send, recv, device):
        return pltpu.make_async_remote_copy(
            src_ref=src, dst_ref=dst, send_sem=send, recv_sem=recv,
            device_id=device, device_id_type=MESH,
        )

    def to_partner(k, atom, src):
        return remote(src, hall.at[atom], sx.at[k], rh.at[atom], partner)

    def along(atom, src, sem, step):
        return remote(src, hall.at[atom], sem, rh.at[atom], {"atom": me + 2 * step, "aux": ax})

    left_ok, right_ok = hi > 0, hi < planes - 1

    @pl.when(left_ok)
    def _():
        along(me, h_ref, sz0.at[0], -1).start()

    @pl.when(right_ok)
    def _():
        along(me, h_ref, sz0.at[1], 1).start()

    to_partner(0, me, h_ref).start()
    for d in range(1, ys):
        remote(h_ref, hx.at[ax], sa.at[d], ra.at[ax], {"atom": me, "aux": ((y + d) % ys) * 2 + c}).start()
    remote(h_ref, hx.at[ax], sa.at[0], ra.at[ax], peer).start()
    own = pltpu.make_async_copy(h_ref, hall.at[me], local_sem.at[0])
    own.start()
    own_aux = pltpu.make_async_copy(h_ref, hx.at[ax], local_sem.at[1])
    own_aux.start()

    def plane_of(k):
        half = (k + 1) // 2
        return hi + half * (1 - 2 * (k % 2))

    def valid(k):
        p = plane_of(k)
        return (p >= 0) & (p < planes) & (k < 2 * planes - 1)

    def forward_ok(k):
        target = hi - (1 - 2 * (k % 2))
        return valid(k) & (target >= 0) & (target < planes)

    def wait_block(atom):
        remote(h_ref, hall.at[atom], sx.at[0], rh.at[atom], partner).wait_recv()

    def relay(k):
        @pl.when(valid(k))
        def _():
            atom = plane_of(k) * 2 + lo
            wait_block(atom)

            @pl.when(forward_ok(k))
            def _():
                along(atom, hall.at[atom], sz.at[k], -(1 - 2 * (k % 2))).start()

            to_partner(k, atom, hall.at[atom]).start()

    relay(1)
    relay(2)

    for d in range(1, ys):
        src = ((y + d) % ys) * 2 + c
        remote(h_ref, hx.at[src], sa.at[0], ra.at[src], peer).wait_recv()
        remote(hx.at[src], hx.at[src], sa.at[ys - 1 + d], ra.at[src], peer).start()
    for d in range(ys):
        src = ((y + d) % ys) * 2 + 1 - c
        remote(h_ref, hx.at[src], sa.at[0], ra.at[src], peer).wait_recv()
    own_aux.wait()
    own.wait()

    piece = 32

    @pl.loop(0, rows // piece)
    def _(j):
        at = pl.ds(pl.multiple_of(j * piece, piece), piece)
        sums = [jnp.zeros((piece, occ), jnp.float32) for _ in range(aux_here)]
        for p in range(aux_here * auxes):
            block = hx[p // aux_here, p % aux_here, at, :].astype(jnp.float32)
            for q in range(aux_here):
                sums[q] = sums[q] + fit_ref[q, p] * block
        for q in range(aux_here):
            g[at, q * occ:(q + 1) * occ] = sums[q].astype(jnp.bfloat16)

    width = 256

    def product(k):
        p = plane_of(k)

        @pl.when(k > 0)
        def _():
            wait_block(p * 2 + 1 - lo)

        @pl.when(k == 0)
        def _():
            wait_block(hi * 2 + 1 - lo)

        for half in range(2):
            @pl.loop(0, rows // width)
            def _(j):
                at = pl.ds(pl.multiple_of(j * width, width), width)
                right = jnp.concatenate(
                    [hall[p * 2 + half, q, at, :] for q in range(aux_here)], axis=-1
                )
                part = lax.dot_general(
                    g[...], right, (((1,), (1,)), ((), ())), preferred_element_type=jnp.float32
                )
                col = pl.ds(pl.multiple_of(half * rows + j * width, width), width)
                epart[p, :, col] = part.astype(jnp.bfloat16)

        @pl.when(p % 2 != c)
        def _():
            remote(epart.at[p], cbuf.at[p // 2], sc.at[p // 2], rc.at[p // 2], peer).start()

    def join(k):
        p = plane_of(k)
        yt = p // 2

        @pl.when(p % 2 == c)
        def _():
            remote(epart.at[p], cbuf.at[yt], sc.at[yt], rc.at[yt], peer).wait_recv()

            @pl.when(yt != y)
            def _():
                @pl.loop(0, rows // 64)
                def _(j):
                    at = pl.ds(pl.multiple_of(j * 64, 64), 64)
                    total = epart[p, at, :].astype(jnp.float32) + cbuf[yt, at, :].astype(jnp.float32)
                    epart[p, at, :] = total.astype(jnp.bfloat16)

                remote(epart.at[p], ybuf.at[y], sy.at[yt], ry.at[y], {"atom": me, "aux": p}).start()

    @pl.loop(0, 2 * planes)
    def _(k):
        @pl.when(valid(k))
        def _():
            product(k)

        @pl.when(k > 0)
        def _():
            @pl.when(valid(k - 1))
            def _():
                join(k - 1)

        relay(k + 3)

    for d in range(1, ys):
        src = (y + d) % ys
        remote(epart.at[ax], ybuf.at[src], sy.at[src], ry.at[src], peer).wait_recv()

    @pl.loop(0, rows // 64)
    def _(j):
        at = pl.ds(pl.multiple_of(j * 64, 64), 64)
        total = epart[ax, at, :].astype(jnp.float32) + cbuf[y, at, :].astype(jnp.float32)
        for d in range(1, ys):
            total = total + ybuf[(y + d) % ys, at, :].astype(jnp.float32)
        out_ref[at, :] = total

    @pl.when(left_ok)
    def _():
        along(me, h_ref, sz0.at[0], -1).wait_send()

    @pl.when(right_ok)
    def _():
        along(me, h_ref, sz0.at[1], 1).wait_send()

    for k in range(2 * planes - 1):
        @pl.when(valid(k))
        def _():
            to_partner(k, me, h_ref).wait_send()

            if k > 0:
                @pl.when(forward_ok(k))
                def _():
                    along(me, h_ref, sz.at[k], -(1 - 2 * (k % 2))).wait_send()

    for d in range(2 * ys - 1):
        remote(h_ref, hx.at[ax], sa.at[d], ra.at[ax], peer).wait_send()
    for t in range(ys):
        remote(epart.at[ax], cbuf.at[t], sc.at[t], rc.at[t], peer).wait_send()
    for d in range(1, ys):
        remote(epart.at[ax], ybuf.at[y], sy.at[(y + d) % ys], ry.at[y], peer).wait_send()


def exchange_call(h, fit_rows):
    aux_here, rows, occ = h.shape
    atoms, auxes = lax.axis_size("atom"), lax.axis_size("aux")
    planes, ys = atoms // 2, auxes // 2
    columns = rows * atoms // auxes
    dma = pltpu.SemaphoreType.DMA
    return pl.pallas_call(
        functools.partial(exchange_kernel, atoms, auxes),
        out_shape=jax.ShapeDtypeStruct((rows, columns), jnp.float32),
        in_specs=[
            pl.BlockSpec(memory_space=pltpu.VMEM),
            pl.BlockSpec(memory_space=pltpu.SMEM),
        ],
        out_specs=pl.BlockSpec(memory_space=pltpu.VMEM),
        scratch_shapes=[
            pltpu.VMEM((atoms, aux_here, rows, occ), jnp.bfloat16),
            pltpu.VMEM((auxes, aux_here, rows, occ), jnp.bfloat16),
            pltpu.VMEM((rows, aux_here * occ), jnp.bfloat16),
            pltpu.VMEM((auxes, rows, columns), jnp.bfloat16),
            pltpu.VMEM((ys, rows, columns), jnp.bfloat16),
            pltpu.VMEM((ys, rows, columns), jnp.bfloat16),
            dma((2,)),
            dma((2 * planes - 1,)),
            dma((2,)),
            dma((2 * planes - 1,)),
            dma((atoms,)),
            dma((2 * ys - 1,)),
            dma((auxes,)),
            dma((ys,)),
            dma((ys,)),
            dma((ys,)),
            dma((ys,)),
        ],
        compiler_params=pltpu.CompilerParams(
            collective_id=0, has_side_effects=True, vmem_limit_bytes=60 * 1024 * 1024
        ),
    )(h, fit_rows)


def route_kernel(
    atoms, order_ref, nu_ref, three_ref, mask_ref, code_ref, own_ref, out_ref,
    orbitals, outgoing, arrived, codes, acc, summed, landed,
    local_sem, sx, sz0, sz, rh, sd, rd, sk, rk, cross_sem,
):
    planes, middle = atoms // 2, atoms // 2
    cap = code_ref.shape[1]
    per, size, occ = own_ref.shape
    aux_here = three_ref.shape[1]
    share = aux_here // 2
    me = lax.axis_index("atom")
    ax = lax.axis_index("aux")
    hi, lo = me // 2, me % 2
    side, pos = me // middle, me % middle

    def at_atom(atom):
        return {"atom": atom, "aux": ax}

    barrier = pltpu.get_barrier_semaphore()
    for d in range(1, atoms):
        pl.semaphore_signal(
            barrier, inc=1, device_id=at_atom((me + d) % atoms), device_id_type=MESH
        )
    pl.semaphore_wait(barrier, atoms - 1)

    def remote(src, dst, send, recv, device):
        return pltpu.make_async_remote_copy(
            src_ref=src, dst_ref=dst, send_sem=send, recv_sem=recv,
            device_id=device, device_id_type=MESH,
        )

    def spot(atom):
        return orbitals.at[pl.ds(atom * per, per)]

    def to_partner(k, atom, src):
        return remote(src, spot(atom), sx.at[k], rh.at[atom], at_atom(hi * 2 + 1 - lo))

    def along(atom, src, sem, step):
        return remote(src, spot(atom), sem, rh.at[atom], at_atom(me + 2 * step))

    left_ok, right_ok = hi > 0, hi < planes - 1

    @pl.when(left_ok)
    def _():
        along(me, own_ref, sz0.at[0], -1).start()

    @pl.when(right_ok)
    def _():
        along(me, own_ref, sz0.at[1], 1).start()

    to_partner(0, me, own_ref).start()
    own = pltpu.make_async_copy(own_ref, spot(me), local_sem.at[0])
    own.start()

    def plane_of(k):
        half = (k + 1) // 2
        return hi + half * (1 - 2 * (k % 2))

    def valid(k):
        p = plane_of(k)
        return (p >= 0) & (p < planes)

    def forward_ok(k):
        target = hi - (1 - 2 * (k % 2))
        return valid(k) & (target >= 0) & (target < planes)

    def wait_block(atom):
        remote(own_ref, spot(atom), sx.at[0], rh.at[atom], at_atom(hi * 2 + 1 - lo)).wait_recv()

    @pl.loop(1, 2 * planes - 1)
    def _(k):
        @pl.when(valid(k))
        def _():
            atom = plane_of(k) * 2 + lo
            wait_block(atom)

            @pl.when(forward_ok(k))
            def _():
                along(atom, spot(atom), sz.at[k], -(1 - 2 * (k % 2))).start()

            to_partner(k, atom, spot(atom)).start()

    @pl.loop(0, planes)
    def _(p):
        wait_block(p * 2 + 1 - lo)

    own.wait()

    def half_block(place, part):
        slot, nu = order_ref[place], nu_ref[place]
        right = orbitals[nu]
        left = three_ref[slot, part * share:(part + 1) * share] * mask_ref[slot][None, :, :]
        value = jnp.dot(
            left.reshape(share * size, size), right, preferred_element_type=jnp.float32
        )
        return value.reshape(share, size, occ).astype(jnp.bfloat16)

    def target_of(j):
        return (pos + j % (middle - 1) + 1) % middle

    def block(part, j, lane, device):
        return remote(
            outgoing.at[part, j], arrived.at[part, lane], sd.at[part, j], rd.at[part, lane], device
        )

    def start_sends(first, owner_side, part):
        @pl.loop(first, first + middle - 1)
        def _(j):
            q = target_of(j)
            owner = owner_side * middle + q
            lane = (first // (middle - 1)) * middle + pos

            @pl.loop(0, cap)
            def _(r):
                outgoing[part, j, r] = half_block(owner * cap + r, part)

            device = at_atom(side * middle + q)
            if part == 0:
                remote(code_ref.at[owner], codes.at[lane], sk.at[j], rk.at[lane], device).start()
            block(part, j, lane, device).start()

    def fill_own(lane, owner, sem):
        @pl.loop(0, cap)
        def _(r):
            for part in range(2):
                arrived[part, lane, r] = half_block(owner * cap + r, part)

        keep = pltpu.make_async_copy(code_ref.at[owner], codes.at[lane], sem)
        keep.start()
        keep.wait()

    start_sends(0, 1 - side, 0)
    start_sends(0, 1 - side, 1)
    fill_own(pos, (1 - side) * middle + pos, local_sem.at[1])
    start_sends(middle - 1, side, 0)
    start_sends(middle - 1, side, 1)
    fill_own(middle + pos, me, local_sem.at[2])

    def take(src, part):
        hits = [
            [codes[src, r, b] for r in range(cap)]
            for b in range(per)
        ]

        @pl.loop(0, share * (size // 64))
        def _(n):
            p, row = n // (size // 64), n % (size // 64)
            at = pl.ds(pl.multiple_of(row * 64, 64), 64)
            values = [
                arrived[part, src, r, p, at, :].astype(jnp.float32).reshape(8, 8, occ)
                for r in range(cap)
            ]
            for b in range(per):
                to = pl.ds(pl.multiple_of(b * size + row * 64, 64), 64)
                total = acc[part * share + p, to, :].reshape(8, 8, occ)
                for r in range(cap):
                    total = total + values[r] * hits[b][r][None]
                acc[part * share + p, to, :] = total.reshape(64, occ)

    def take_all(base, part):
        span = pl.ds(part * share, share)
        acc[span] = jnp.zeros((share,) + acc.shape[1:], jnp.float32)
        take(base + pos, part)

        @pl.loop(1, middle)
        def _(i):
            src = (pos + middle - i) % middle
            lane = base + src
            device = at_atom(side * middle + src)
            if part == 0:
                remote(code_ref.at[0], codes.at[lane], sk.at[0], rk.at[lane], device).wait_recv()
            block(part, 0, lane, device).wait_recv()
            take(lane, part)

    across = at_atom((1 - side) * middle + pos)
    crossings = []
    for part in range(2):
        take_all(0, part)
        span = pl.ds(part * share, share)
        summed[span] = acc[span].astype(jnp.bfloat16)
        cross = remote(
            summed.at[span], landed.at[span], cross_sem.at[part], cross_sem.at[2 + part], across
        )
        cross.start()
        crossings.append(cross)
    take_all(middle, 0)
    take_all(middle, 1)
    for part in range(2):
        crossings[part].wait_recv()
        span = pl.ds(part * share, share)
        out_ref[span] = (acc[span] + landed[span].astype(jnp.float32)).astype(jnp.bfloat16)
    for cross in crossings:
        cross.wait_send()

    @pl.when(left_ok)
    def _():
        along(me, own_ref, sz0.at[0], -1).wait_send()

    @pl.when(right_ok)
    def _():
        along(me, own_ref, sz0.at[1], 1).wait_send()

    to_partner(0, me, own_ref).wait_send()

    @pl.loop(1, 2 * planes - 1)
    def _(k):
        @pl.when(valid(k))
        def _():
            to_partner(k, me, own_ref).wait_send()

            @pl.when(forward_ok(k))
            def _():
                along(me, own_ref, sz.at[k], -(1 - 2 * (k % 2))).wait_send()

    @pl.loop(0, 2 * middle - 2)
    def _(j):
        device = at_atom(side * middle + target_of(j))
        block(0, j, 0, device).wait_send()
        block(1, j, 0, device).wait_send()
        remote(code_ref.at[0], codes.at[0], sk.at[j], rk.at[0], device).wait_send()


def route_call(order, nu, three_index, mask, codes, coefficients):
    aux_here, size = three_index.shape[1], three_index.shape[2]
    rows, occ = coefficients.shape
    per = rows // size
    atoms = lax.axis_size("atom")
    planes = atoms // 2
    dma = pltpu.SemaphoreType.DMA
    smem = pl.BlockSpec(memory_space=pltpu.SMEM)
    vmem = pl.BlockSpec(memory_space=pltpu.VMEM)
    return pl.pallas_call(
        functools.partial(route_kernel, atoms),
        out_shape=jax.ShapeDtypeStruct((aux_here, rows, occ), jnp.bfloat16),
        in_specs=[smem, smem, vmem, vmem, vmem, vmem],
        out_specs=vmem,
        scratch_shapes=[
            pltpu.VMEM((atoms * per, size, occ), jnp.bfloat16),
            pltpu.VMEM((2, atoms - 2, CAP, aux_here // 2, size, occ), jnp.bfloat16),
            pltpu.VMEM((2, atoms, CAP, aux_here // 2, size, occ), jnp.bfloat16),
            pltpu.VMEM((atoms, CAP, per, 8, 128), jnp.float32),
            pltpu.VMEM((aux_here, rows, occ), jnp.float32),
            pltpu.VMEM((aux_here, rows, occ), jnp.bfloat16),
            pltpu.VMEM((aux_here, rows, occ), jnp.bfloat16),
            dma((3,)),
            dma((2 * planes - 1,)),
            dma((2,)),
            dma((2 * planes - 1,)),
            dma((atoms,)),
            dma((2, atoms - 2)),
            dma((2, atoms)),
            dma((atoms - 2,)),
            dma((atoms,)),
            dma((4,)),
        ],
        compiler_params=pltpu.CompilerParams(
            collective_id=1, has_side_effects=True, vmem_limit_bytes=60 * 1024 * 1024
        ),
    )(order, nu, three_index, mask, codes, coefficients.reshape(per, size, occ))


def per_device(
    three_index, pair_mask, pair_owner, pair_sub, pair_nu, live_count, coefficients, fit_matrix
):
    slot_count, aux_here, block_size, _ = three_index.shape
    rows_here, occupied = coefficients.shape
    atom_count = lax.axis_size("atom")
    aux_total = fit_matrix.shape[1]
    shell_size = block_size // pair_mask.shape[1]
    expanded = jnp.repeat(jnp.repeat(pair_mask, shell_size, 1), shell_size, 2).astype(jnp.bfloat16)
    owners = pair_owner[:, 0]
    owner_hits = (owners[:, None] == jnp.arange(atom_count)[None, :]).astype(jnp.int32)
    rank_within = jnp.sum(jnp.cumsum(owner_hits, 0) * owner_hits, 1) - 1
    placement = owners * CAP + rank_within
    routing = (jnp.arange(atom_count * CAP)[:, None] == placement[None, :]).astype(jnp.int32)
    slots = jnp.arange(slot_count, dtype=jnp.int32)

    def placed(values):
        return jnp.sum(routing * values[None, :], 1)

    live_codes = placed(jnp.where(slots < live_count[0], pair_sub + 1, 0))
    blocks = jnp.arange(rows_here // block_size)
    hits = (live_codes[:, None] == blocks[None, :] + 1).astype(jnp.float32)
    hits = hits.reshape(atom_count, CAP, blocks.shape[0], 1, 1)
    local_rows = route_call(
        placed(slots),
        placed(pair_nu),
        three_index,
        expanded,
        jnp.broadcast_to(hits, hits.shape[:3] + (8, 128)),
        coefficients,
    )
    total = exchange_call(local_rows, fit_matrix.astype(jnp.float32))
    return total * (aux_total * occupied) ** (-0.5)


def solution(mesh):
    in_specs = (
        P("atom", "aux", None, None),
        P("atom", None, None),
        P("atom", None),
        P("atom"),
        P("atom"),
        P("atom"),
        P("atom", None),
        P("aux", None),
    )
    out_specs = P("atom", "aux")
    return jax.shard_map(
        per_device, mesh=mesh, in_specs=in_specs, out_specs=out_specs, check_vma=False
    )
```

profile of v0, /device:TPU:5, one launch (start us, length us, event | category | flops | bytes accessed | tf_op | source)
XLA Modules:
  0.0 220.6 jit_solution(6628303083012027195)
XLA Ops:
  0.7 1.3 convert_element_type.26.fit_ref
  1.9 0.7 fusion
  2.7 0.8 select_reduce_fusion.3
  3.5 0.7 compare_select_fusion
  4.2 1.3 select_reduce_fusion
  5.6 0.1 eq.51
  5.6 0.1 compare_convert_fusion
  5.7 0.8 convert_element_type.22
  6.5 0.1 copy.12
  6.6 0.2 broadcast_in_dim.10
  6.8 0.2 convert_element_type.23
  7.0 0.8 broadcast_in_dim.13.code_ref
  7.8 0.1 broadcast_in_dim.11
  7.9 1.0 copy.13.mask_ref
  8.9 86.7 %shard_map.82.h_ref = bf16[8,512,128]{2,1,0:T(8,128)(2,1)} custom-call(s32[16]{0:T(128)} %get-tuple-element.7.order_ref, s32[16]{0:T(128)} %get-tuple-element.6.nu_ref, bf16[16,8,128,128]{3,2,1,0:T(8,128)(2,1)} %three_ref.1, bf16[16,128,128]{2,1,0:T(8,128)(2,1)} %copy.13.mask_ref, f32[8,2,4,8,128]{4,3,2,1,0:T(8,128)} %broadcast_in_dim.13.code_ref, ...), custom_call_target="tpu_custom_call" | custom-call | tf_op jit(solution)/shard_map/pallas_call | solution.py:504
  95.7 121.8 %shard_map.83 = f32[512,1024]{1,0:T(8,128)} custom-call(bf16[8,512,128]{2,1,0:T(8,128)(2,1)} %shard_map.82.h_ref, f32[8,32]{1,0:T(8,128)} %convert_element_type.26.fit_ref), custom_call_target="tpu_custom_call" | custom-call | tf_op jit(solution)/shard_map/pallas_call | solution.py:240
  217.4 3.2 %broadcast_multiply_fusion = f32[512,1024]{1,0:T(8,128)} fusion(f32[512,1024]{1,0:T(8,128)} %shard_map.83), kind=kLoop, calls=%fused_computation | loop fusion | flops 524288 | bytes 4194304 | tf_op jit(solution)/shard_map/mul | solution.py:566
  (2 shorter events, 0.0 us)
where the time goes:
time: 221 us
  Pallas kernels  208 us (94%)
  other arithmetic  8.97 us (4%)
  local copies, waits for them, and re-layouts  2.48 us (1%)
    pallas_call x1, Pallas kernels, exchange_call(): pl.pallas_call(functools.partial(exchange_kernel, atoms, auxes), out_shap...  122 us
    pallas_call x1, Pallas kernels, route_call(): pl.pallas_call(functools.partial(route_kernel, atoms), out_shape=jax.Shap...  86.7 us

commit v1 on v0

--- a/solution.py
+++ b/solution.py
@@ -1,4 +1,5 @@
 import functools
+import math
 
 import jax
 import jax.numpy as jnp
@@ -531,6 +532,655 @@
     )(order, nu, three_index, mask, codes, coefficients.reshape(per, size, occ))
 
 
+def fused_kernel(
+    planes, auxes, step,
+    owner_ref, sub_ref, nu_ref, live_ref, three_hbm, mask_ref, coef_ref, kron_ref, out_ref,
+    three, mexp, mrows, orb, order, nus, hits, hits_in, keep, xs, xr, up, dn, zb, own_rows, rows_all, fitted, kron, cs, cr,
+    local_sem, orb_recv, orb_own, orb_line, orb_x, orb_core, code_sem, kron_send, kron_recv,
+    x_send, x_recv, up_send, up_recv, dn_send, dn_recv,
+    own_sem, line_up, line_dn, line_recv, b_send, b_recv, a_send, a_recv, c_send, c_recv,
+):
+    slot_count, aux_here, size, _ = three_hbm.shape
+    per = coef_ref.shape[0]
+    rows, occ = per * size, coef_ref.shape[2]
+    atoms = planes * 2
+    half = per // 2
+    chunks = aux_here // step
+    shells = mask_ref.shape[1]
+    shell = size // shells
+    me = lax.axis_index("atom")
+    ax = lax.axis_index("aux")
+    z, x = me // 2, me % 2
+    y, c = ax // 2, ax % 2
+    ys = auxes // 2
+    above, below = {"atom": me + 2, "aux": ax}, {"atom": me - 2, "aux": ax}
+    partner = {"atom": z * 2 + 1 - x, "aux": ax}
+    core = {"atom": me, "aux": y * 2 + 1 - c}
+    has_up, has_dn = z < planes - 1, z > 0
+
+    def at_aux(u):
+        return {"atom": me, "aux": u}
+
+    barrier = pltpu.get_barrier_semaphore()
+
+    def greet(device):
+        pl.semaphore_signal(barrier, inc=1, device_id=device, device_id_type=MESH)
+
+    greet(partner)
+    for d in range(1, auxes):
+        greet(at_aux((ax + d) % auxes))
+
+    @pl.when(has_up)
+    def _():
+        greet(above)
+
+    @pl.when(has_dn)
+    def _():
+        greet(below)
+
+    load_three = pltpu.make_async_copy(three_hbm, three, local_sem.at[0])
+    load_three.start()
+    load_kron = pltpu.make_async_copy(
+        kron_ref, kron.at[pl.ds(pl.multiple_of(ax * kron_ref.shape[0], kron_ref.shape[0]), kron_ref.shape[0])], local_sem.at[1]
+    )
+    load_kron.start()
+    load_orb = pltpu.make_async_copy(coef_ref, orb.at[pl.ds(me * per, per)], local_sem.at[2])
+    load_orb.start()
+
+    pl.semaphore_wait(
+        barrier, auxes + jnp.minimum(z, 1) + jnp.minimum(planes - 1 - z, 1)
+    )
+
+    def remote(src, dst, send, recv, device):
+        return pltpu.make_async_remote_copy(
+            src_ref=src, dst_ref=dst, send_sem=send, recv_sem=recv,
+            device_id=device, device_id_type=MESH,
+        )
+
+    def spot(atom, part):
+        return orb.at[pl.ds(atom * per + part * half, half)]
+
+    own_part = coef_ref.at[pl.ds(c * half, half)]
+
+    def orb_copy(src, atom, part, send, device):
+        return remote(src, spot(atom, part), send, orb_recv.at[atom * 2 + part], device)
+
+    @pl.when(has_up)
+    def _():
+        orb_copy(own_part, me, c, orb_own.at[0], above).start()
+
+    @pl.when(has_dn)
+    def _():
+        orb_copy(own_part, me, c, orb_own.at[1], below).start()
+
+    orb_copy(own_part, me, c, orb_own.at[2], partner).start()
+
+    def wait_orb(atom, part):
+        orb_copy(own_part, atom, part, orb_own.at[0], partner).wait_recv()
+
+    lane_row = lax.broadcasted_iota(jnp.int32, (8, 128), 0)
+    live = live_ref[0]
+
+    @pl.loop(0, atoms)
+    def _(o):
+        def scan(s, carry):
+            count, slots, nu, codes = carry
+            hit = owner_ref[s] == o
+            code = jnp.where(s < live, sub_ref[s] + 1, 0)
+            new = []
+            for r in range(CAP):
+                take = hit & (count == r)
+                new.append((
+                    jnp.where(take, s, slots[r]),
+                    jnp.where(take, nu_ref[s], nu[r]),
+                    jnp.where(take, code, codes[r]),
+                ))
+            count = count + jnp.where(hit, 1, 0)
+            return count, tuple(v[0] for v in new), tuple(v[1] for v in new), tuple(v[2] for v in new)
+
+        zero = jnp.int32(0)
+        zeros = (zero,) * CAP
+        _, slots, nu, codes = lax.fori_loop(0, slot_count, scan, (zero, zeros, zeros, zeros))
+        for r in range(CAP):
+            index = ((o % 2) * planes + o // 2) * CAP + r
+            order[index] = slots[r]
+            nus[index] = nu[r]
+            hits[index] = jnp.where(lane_row == codes[r] - 1, 1.0, 0.0)
+
+    code_count = planes * CAP
+    send_codes = remote(
+        hits.at[pl.ds((1 - x) * code_count, code_count)], hits_in, code_sem.at[0], code_sem.at[1], partner
+    )
+    send_codes.start()
+
+    spread = jnp.where(
+        lax.broadcasted_iota(jnp.int32, (shells, size), 1) // shell
+        == lax.broadcasted_iota(jnp.int32, (shells, size), 0), 1.0, 0.0
+    )
+    mrows[...] = jnp.dot(
+        mask_ref[...].astype(jnp.float32), spread, preferred_element_type=jnp.float32
+    )
+
+    @pl.loop(0, slot_count)
+    def _(s):
+        small = mrows[pl.ds(pl.multiple_of(s * shells, shells), shells), :]
+        for j in range(shells):
+            mexp[s, j * shell:(j + 1) * shell, :] = jnp.broadcast_to(
+                small[j:j + 1, :], (shell, size)
+            ).astype(jnp.bfloat16)
+
+    def pass_orb(p, upward):
+        atom = p * 2 + x
+        wait_orb(atom, c)
+        if upward:
+            @pl.when(has_up)
+            def _():
+                orb_copy(spot(atom, c), atom, c, orb_line.at[p], above).start()
+        else:
+            @pl.when(has_dn)
+            def _():
+                orb_copy(spot(atom, c), atom, c, orb_line.at[p], below).start()
+        orb_copy(spot(atom, c), atom, c, orb_x.at[p], partner).start()
+        orb_copy(spot(atom, c), atom, c, orb_core.at[atom], core).start()
+
+    def hand_orb(p):
+        atom = p * 2 + 1 - x
+        wait_orb(atom, c)
+        orb_copy(spot(atom, c), atom, c, orb_core.at[atom], core).start()
+
+    @pl.loop(1, planes)
+    def _(d):
+        @pl.when(z - d >= 0)
+        def _():
+            pass_orb(z - d, True)
+
+        @pl.when(z + d < planes)
+        def _():
+            pass_orb(z + d, False)
+
+    hand_orb(z)
+
+    @pl.loop(1, planes)
+    def _(d):
+        @pl.when(z - d >= 0)
+        def _():
+            hand_orb(z - d)
+
+        @pl.when(z + d < planes)
+        def _():
+            hand_orb(z + d)
+
+    load_kron.wait()
+    load_orb.wait()
+
+    def kron_part(u):
+        return kron.at[pl.ds(pl.multiple_of(u * kron_ref.shape[0], kron_ref.shape[0]), kron_ref.shape[0])]
+
+    for d in range(1, auxes):
+        remote(kron_ref, kron_part(ax), kron_send.at[d], kron_recv.at[ax], at_aux((ax + d) % auxes)).start()
+
+    @pl.loop(0, planes)
+    def _(p):
+        wait_orb(p * 2 + 1 - x, 1 - c)
+
+        @pl.when(p != z)
+        def _():
+            wait_orb(p * 2 + x, 1 - c)
+
+    load_three.wait()
+    send_codes.wait_recv()
+
+    def half_block(index, k):
+        slot, nu = order[index], nus[index]
+        left = three[slot, pl.ds(k * step, step)] * mexp[slot][None, :, :]
+        value = jnp.dot(
+            left.reshape(step * size, size), orb[nu], preferred_element_type=jnp.float32
+        )
+        return value.reshape(step, size, occ).astype(jnp.bfloat16)
+
+    def span(k):
+        return pl.ds(k * step, step)
+
+    def x_copy(k):
+        return remote(xs.at[k], xr.at[k], x_send.at[k], x_recv.at[k], partner)
+
+    def add_dense(p, k, extras, target):
+        own_hits = [
+            [jnp.broadcast_to(hits[(x * planes + p) * CAP + r, b:b + 1, :], (8, 128))[None] for r in range(CAP)]
+            for b in range(per)
+        ]
+        in_hits = [
+            [jnp.broadcast_to(hits_in[p * CAP + r, b:b + 1, :], (8, 128))[None] for r in range(CAP)]
+            for b in range(per)
+        ]
+        strip = 64
+
+        def strips(j, place, row):
+            at = pl.ds(pl.multiple_of(row * strip, strip), strip)
+            shape = (strip // 8, 8, occ)
+            own = [keep[k, p, r, j, at, :].astype(jnp.float32).reshape(shape) for r in range(CAP)]
+            other = [xr[k, p, r, j, at, :].astype(jnp.float32).reshape(shape) for r in range(CAP)]
+            for b in range(per):
+                to = pl.ds(pl.multiple_of(b * size + row * strip, strip), strip)
+                total = own[0] * own_hits[b][0] + other[0] * in_hits[b][0]
+                for r in range(1, CAP):
+                    total = total + own[r] * own_hits[b][r] + other[r] * in_hits[b][r]
+                for extra in extras:
+                    total = total + extra[p, place, to, :].astype(jnp.float32).reshape(shape)
+                value = total.reshape(strip, occ).astype(jnp.bfloat16)
+                if target is own_rows:
+                    target[place, to, :] = value
+                else:
+                    target[p, place, to, :] = value
+
+        for j in range(step):
+            place = k if step == 1 else k * step + j
+
+            @pl.loop(0, size // strip)
+            def _(row):
+                strips(j, place, row)
+
+    def up_copy(p, k):
+        ref = up.at[p, span(k)]
+        return remote(ref, ref, up_send.at[p, k], up_recv.at[p, k], above)
+
+    def dn_copy(p, k):
+        ref = dn.at[p, span(k)]
+        return remote(ref, ref, dn_send.at[p, k], dn_recv.at[p, k], below)
+
+    def lane_of(p):
+        return (p + 2 * planes - ax - 1) % planes
+
+    def b_lane(sender, target):
+        return planes - 1 + (sender + auxes - target) % auxes
+
+    def line_copy(src, p, k, send, device):
+        return remote(src, zb.at[lane_of(p), span(k)], send, line_recv.at[p, k], device)
+
+    def b_copy(src, p, k):
+        return remote(src, zb.at[b_lane(ax, p), span(k)], b_send.at[p, k], b_recv.at[ax, k], at_aux(p))
+
+    def a_piece(column, u, k):
+        return rows_all.at[column, u, span(k)]
+
+    def a_copy(column, u, k, which, device):
+        ref = a_piece(column, u, k)
+        return remote(ref, ref, a_send.at[which, k], a_recv.at[column, u, k], device)
+
+    def own_a_copy(k, which, device):
+        return remote(
+            own_rows.at[span(k)], a_piece(x, ax, k), a_send.at[which, k], a_recv.at[x, ax, k], device
+        )
+
+    def own_copy(k):
+        return pltpu.make_async_copy(own_rows.at[span(k)], a_piece(x, ax, k), own_sem.at[k])
+
+    def y_devices():
+        return [((y + d) % ys) * 2 + c for d in range(1, ys)]
+
+    def inside(k):
+        return (k >= 0) & (k < chunks)
+
+    def reduce_rows(t, zz):
+        if zz < planes - 1:
+            ku = t - 1 - zz
+
+            @pl.when(inside(ku))
+            def _():
+                for p in range(planes - 1, zz, -1):
+                    if zz > 0:
+                        up_copy(p, ku).wait_recv()
+                    add_dense(p, ku, [up] if zz > 0 else [], up)
+                    up_copy(p, ku).start()
+
+        if zz > 0:
+            kd = t - planes + zz
+
+            @pl.when(inside(kd))
+            def _():
+                for p in range(zz):
+                    if zz < planes - 1:
+                        dn_copy(p, kd).wait_recv()
+                    add_dense(p, kd, [dn] if zz < planes - 1 else [], dn)
+                    dn_copy(p, kd).start()
+
+        kh = t - 1 - max(zz, planes - 1 - zz)
+
+        @pl.when(inside(kh))
+        def _():
+            extras = []
+            if zz > 0:
+                up_copy(zz, kh).wait_recv()
+                extras.append(up)
+            if zz < planes - 1:
+                dn_copy(zz, kh).wait_recv()
+                extras.append(dn)
+            add_dense(zz, kh, extras, own_rows)
+            mine = own_rows.at[span(kh)]
+            own_copy(kh).start()
+            if zz < planes - 1:
+                line_copy(mine, zz, kh, line_up.at[zz, kh], above).start()
+            if zz > 0:
+                line_copy(mine, zz, kh, line_dn.at[zz, kh], below).start()
+            own_a_copy(kh, 0, partner).start()
+            for n, u in enumerate(y_devices()):
+                own_a_copy(kh, 7 + 2 * n, at_aux(u)).start()
+            own_a_copy(kh, 1, core).start()
+
+    def pass_line(t, zz, p):
+        kz = t - 1 - max(p, planes - 1 - p) - abs(zz - p)
+
+        @pl.when(inside(kz))
+        def _():
+            piece = zb.at[lane_of(p), span(kz)]
+            line_copy(piece, p, kz, line_up.at[p, kz], above).wait_recv()
+            if p < zz < planes - 1:
+                line_copy(piece, p, kz, line_up.at[p, kz], above).start()
+            if p > zz > 0:
+                line_copy(piece, p, kz, line_dn.at[p, kz], below).start()
+
+            @pl.when(p != ax)
+            def _():
+                b_copy(piece, p, kz).start()
+
+    def pass_rows(t, zz):
+        for d in range(1, planes):
+            for p in (zz - d, zz + d):
+                if 0 <= p < planes:
+                    pass_line(t, zz, p)
+
+        ka = t - 2 - max(zz, planes - 1 - zz)
+
+        @pl.when(inside(ka))
+        def _():
+            a_copy(1 - x, ax, ka, 0, partner).wait_recv()
+            for n, u in enumerate(y_devices()):
+                a_copy(1 - x, ax, ka, 8 + 2 * n, at_aux(u)).start()
+            a_copy(1 - x, ax, ka, 2, core).start()
+            for n, u in enumerate(y_devices()):
+                a_copy(x, u, ka, 0, partner).wait_recv()
+                a_copy(x, u, ka, 7 + 2 * (ys - 1) + 2 * n, core).start()
+
+        kb = t - 3 - max(zz, planes - 1 - zz)
+
+        @pl.when(inside(kb))
+        def _():
+            for n, u in enumerate(y_devices()):
+                a_copy(1 - x, u, kb, 0, partner).wait_recv()
+                a_copy(1 - x, u, kb, 8 + 2 * (ys - 1) + 2 * n, core).start()
+
+    @pl.loop(0, chunks + 2 * planes - 1)
+    def _(t):
+        @pl.when(t < chunks)
+        def _():
+            @pl.loop(0, planes)
+            def _(p):
+                for r in range(CAP):
+                    xs[t, p, r] = half_block(((1 - x) * planes + p) * CAP + r, t)
+
+            x_copy(t).start()
+
+            @pl.loop(0, planes)
+            def _(p):
+                for r in range(CAP):
+                    keep[t, p, r] = half_block((x * planes + p) * CAP + r, t)
+
+        @pl.when((t >= 1) & (t <= chunks))
+        def _():
+            x_copy(t - 1).wait_recv()
+
+        for zz in range(planes):
+            @pl.when(z == zz)
+            def _():
+                reduce_rows(t, zz)
+                pass_rows(t, zz)
+
+    for d in range(1, auxes):
+        remote(kron_ref, kron_part((ax + d) % auxes), kron_send.at[d], kron_recv.at[(ax + d) % auxes], core).wait_recv()
+
+    @pl.loop(0, chunks)
+    def _(k):
+        own_copy(k).wait()
+        for d in range(ys):
+            u = ((y + d) % ys) * 2 + 1 - c
+            for column in range(2):
+                a_copy(column, u, k, 0, partner).wait_recv()
+
+        @pl.when(z != ax)
+        def _():
+            for d in range(1, auxes):
+                u = (ax + d) % auxes
+                remote(
+                    zb.at[b_lane(u, ax), span(k)], zb.at[b_lane(u, ax), span(k)],
+                    b_send.at[0, k], b_recv.at[u, k], core,
+                ).wait_recv()
+
+    total_aux = auxes * aux_here
+    strip = kron_ref.shape[0] // aux_here
+
+    def mix(load):
+        @pl.loop(0, rows // (2 * strip))
+        def _(j):
+            spots = [
+                pl.ds(pl.multiple_of(j * 2 * strip + h * strip, strip), strip) for h in range(2)
+            ]
+            right = jnp.concatenate(
+                [load(at).reshape(total_aux * strip, occ) for at in spots], axis=-1
+            )
+            value = jnp.dot(kron[...], right, preferred_element_type=jnp.float32).astype(jnp.bfloat16)
+            for h in range(2):
+                for q in range(total_aux):
+                    fitted[spots[h], q * occ:(q + 1) * occ] = value[
+                        q * strip:(q + 1) * strip, h * occ:(h + 1) * occ
+                    ]
+
+    @pl.when(z == ax)
+    def _():
+        mix(lambda at: rows_all[x, :, :, at, :])
+
+    @pl.when(z != ax)
+    def _():
+        mix(lambda at: jnp.concatenate([zb[b_lane(u, ax), :, at, :] for u in range(auxes)], axis=0))
+
+    block = 256
+
+    def product(column, j):
+        at = pl.ds(pl.multiple_of(j * block, block), block)
+        left = jnp.concatenate(
+            [rows_all[column, q // aux_here, q % aux_here, at, :] for q in range(total_aux)], axis=-1
+        )
+        return at, lax.dot_general(
+            left, fitted[...], (((1,), (1,)), ((), ())), preferred_element_type=jnp.float32
+        )
+
+    def c_copy(j):
+        at = pl.ds(pl.multiple_of(j * block, block), block)
+        return remote(cs.at[at], cr.at[at], c_send.at[j], c_recv.at[j], partner)
+
+    @pl.loop(0, rows // block)
+    def _(j):
+        at, value = product(1 - x, j)
+        cs[at, :] = value.astype(jnp.bfloat16)
+        c_copy(j).start()
+
+    @pl.loop(0, rows // block)
+    def _(j):
+        at, value = product(x, j)
+        out_ref[at, pl.ds(pl.multiple_of(x * rows, rows), rows)] = value
+
+    @pl.loop(0, rows // block)
+    def _(j):
+        c_copy(j).wait_recv()
+        at = pl.ds(pl.multiple_of(j * block, block), block)
+        out_ref[at, pl.ds(pl.multiple_of((1 - x) * rows, rows), rows)] = cr[at, :].astype(jnp.float32)
+
+    @pl.when(has_up)
+    def _():
+        orb_copy(own_part, me, c, orb_own.at[0], above).wait_send()
+
+    @pl.when(has_dn)
+    def _():
+        orb_copy(own_part, me, c, orb_own.at[1], below).wait_send()
+
+    orb_copy(own_part, me, c, orb_own.at[2], partner).wait_send()
+    send_codes.wait_send()
+
+    @pl.loop(0, planes)
+    def _(p):
+        @pl.when(p != z)
+        def _():
+            @pl.when(((p < z) & has_up) | ((p > z) & has_dn))
+            def _():
+                orb_copy(own_part, me, c, orb_line.at[p], partner).wait_send()
+
+            orb_copy(own_part, me, c, orb_x.at[p], partner).wait_send()
+            orb_copy(own_part, me, c, orb_core.at[p * 2 + x], partner).wait_send()
+
+        orb_copy(own_part, me, c, orb_core.at[p * 2 + 1 - x], partner).wait_send()
+
+    for d in range(1, auxes):
+        remote(kron_ref, kron_part(ax), kron_send.at[d], kron_recv.at[ax], core).wait_send()
+
+    @pl.loop(0, chunks)
+    def _(k):
+        x_copy(k).wait_send()
+        for which in range(7 + 4 * (ys - 1)):
+            if which < 3 or which >= 7:
+                a_copy(x, ax, k, which, partner).wait_send()
+
+        @pl.loop(0, planes)
+        def _(p):
+            @pl.when(p > z)
+            def _():
+                up_copy(p, k).wait_send()
+
+            @pl.when(p < z)
+            def _():
+                dn_copy(p, k).wait_send()
+
+            @pl.when((p <= z) & has_up)
+            def _():
+                line_copy(a_piece(x, ax, k), z, k, line_up.at[p, k], partner).wait_send()
+
+            @pl.when((p >= z) & has_dn)
+            def _():
+                line_copy(a_piece(x, ax, k), z, k, line_dn.at[p, k], partner).wait_send()
+
+            @pl.when((p != z) & (p != ax))
+            def _():
+                b_copy(a_piece(x, ax, k), p, k).wait_send()
+
+    @pl.loop(0, rows // block)
+    def _(j):
+        c_copy(j).wait_send()
+
+
+def fused_scratch(planes, auxes, step, slot_count, aux_here, size, occ, per, shells, kron_rows):
+    atoms, rows, chunks, ys = planes * 2, per * size, aux_here // step, auxes // 2
+    dma = pltpu.SemaphoreType.DMA
+    half = jnp.bfloat16
+    ways = 7 + 4 * (ys - 1)
+    buffers = [
+        pltpu.VMEM((slot_count, aux_here, size, size), half),
+        pltpu.VMEM((slot_count, size, size), half),
+        pltpu.VMEM((slot_count * shells, size), jnp.float32),
+        pltpu.VMEM((atoms * per, size, occ), half),
+        pltpu.SMEM((atoms * CAP,), jnp.int32),
+        pltpu.SMEM((atoms * CAP,), jnp.int32),
+        pltpu.VMEM((atoms * CAP, 8, 128), jnp.float32),
+        pltpu.VMEM((planes * CAP, 8, 128), jnp.float32),
+        pltpu.VMEM((chunks, planes, CAP, step, size, occ), half),
+        pltpu.VMEM((chunks, planes, CAP, step, size, occ), half),
+        pltpu.VMEM((chunks, planes, CAP, step, size, occ), half),
+        pltpu.VMEM((planes, aux_here, rows, occ), half),
+        pltpu.VMEM((planes, aux_here, rows, occ), half),
+        pltpu.VMEM((planes + auxes - 1, aux_here, rows, occ), half),
+        pltpu.VMEM((aux_here, rows, occ), half),
+        pltpu.VMEM((2, auxes, aux_here, rows, occ), half),
+        pltpu.VMEM((rows, auxes * aux_here * occ), half),
+        pltpu.VMEM((auxes * kron_rows, auxes * kron_rows), half),
+        pltpu.VMEM((rows, rows), half),
+        pltpu.VMEM((rows, rows), half),
+    ]
+    semaphores = [
+        dma((3,)),
+        dma((atoms * 2,)),
+        dma((3,)),
+        dma((planes,)),
+        dma((planes,)),
+        dma((atoms,)),
+        dma((2,)),
+        dma((auxes,)),
+        dma((auxes,)),
+        dma((chunks,)),
+        dma((chunks,)),
+        dma((planes, chunks)),
+        dma((planes, chunks)),
+        dma((planes, chunks)),
+        dma((planes, chunks)),
+        dma((chunks,)),
+        dma((planes, chunks)),
+        dma((planes, chunks)),
+        dma((planes, chunks)),
+        dma((planes, chunks)),
+        dma((auxes, chunks)),
+        dma((ways, chunks)),
+        dma((2, auxes, chunks)),
+        dma((rows // 256,)),
+        dma((rows // 256,)),
+    ]
+    return buffers, semaphores
+
+
+VMEM_LIMIT = 60 * 1024 * 1024
+STRIP = 16
+
+
+def fused_plan(planes, auxes, three_index, pair_mask, coefficients):
+    slot_count, aux_here, size, _ = three_index.shape
+    rows, occ = coefficients.shape
+    per, shells = rows // size, pair_mask.shape[1]
+    if planes != auxes or per % 2 or per > 8 or rows % 256 or shells % 8:
+        return None
+    step = 1
+    buffers, semaphores = fused_scratch(
+        planes, auxes, step, slot_count, aux_here, size, occ, per, shells, aux_here * STRIP
+    )
+    held = rows * 2 * rows * 4 + 2 * rows * occ * 2
+    for ref in buffers:
+        held += math.prod(ref.shape) * jnp.dtype(ref.dtype).itemsize
+    if held > VMEM_LIMIT - 4 * 1024 * 1024:
+        return None
+    return step, buffers + semaphores
+
+
+def fused_call(plan, planes, auxes, three_index, pair_mask, owners, subs, nus, live, coefficients, fit_rows):
+    step, scratch = plan
+    slot_count, aux_here, size, _ = three_index.shape
+    rows, occ = coefficients.shape
+    shells = pair_mask.shape[1]
+    total_aux = fit_rows.shape[1]
+    width = jnp.repeat(jnp.repeat(fit_rows, STRIP, 0), STRIP, 1)
+    row = lax.broadcasted_iota(jnp.int32, width.shape, 0) % STRIP
+    col = lax.broadcasted_iota(jnp.int32, width.shape, 1) % STRIP
+    kron_rows = jnp.where(row == col, width, jnp.zeros_like(width))
+    smem = pl.BlockSpec(memory_space=pltpu.SMEM)
+    vmem = pl.BlockSpec(memory_space=pltpu.VMEM)
+    return pl.pallas_call(
+        functools.partial(fused_kernel, planes, auxes, step),
+        out_shape=jax.ShapeDtypeStruct((rows, 2 * rows), jnp.float32),
+        in_specs=[smem] * 4 + [pl.BlockSpec(memory_space=pl.ANY)] + [vmem] * 3,
+        out_specs=vmem,
+        scratch_shapes=scratch,
+        compiler_params=pltpu.CompilerParams(
+            collective_id=2, has_side_effects=True, vmem_limit_bytes=VMEM_LIMIT
+        ),
+    )(
+        owners, subs, nus, live, three_index, pair_mask.reshape(slot_count * shells, shells),
+        coefficients.reshape(rows // size, size, occ), kron_rows,
+    )
+
+
 def per_device(
     three_index, pair_mask, pair_owner, pair_sub, pair_nu, live_count, coefficients, fit_matrix
 ):
@@ -538,11 +1188,19 @@
     rows_here, occupied = coefficients.shape
     atom_count = lax.axis_size("atom")
     aux_total = fit_matrix.shape[1]
+    planes, auxes = atom_count // 2, lax.axis_size("aux")
+    plan = fused_plan(planes, auxes, three_index, pair_mask, coefficients)
+    if plan is not None:
+        total = fused_call(
+            plan, planes, auxes, three_index, pair_mask, pair_owner[:, 0], pair_sub, pair_nu,
+            live_count, coefficients, fit_matrix,
+        )
+        return total * (aux_total * occupied) ** (-0.5)
     shell_size = block_size // pair_mask.shape[1]
     expanded = jnp.repeat(jnp.repeat(pair_mask, shell_size, 1), shell_size, 2).astype(jnp.bfloat16)
     owners = pair_owner[:, 0]
-    owner_hits = (owners[:, None] == jnp.arange(atom_count)[None, :]).astype(jnp.int32)
-    rank_within = jnp.sum(jnp.cumsum(owner_hits, 0) * owner_hits, 1) - 1
+    ahead = jnp.arange(slot_count)[None, :] < jnp.arange(slot_count)[:, None]
+    rank_within = jnp.sum(((owners[:, None] == owners[None, :]) & ahead).astype(jnp.int32), 1)
     placement = owners * CAP + rank_within
     routing = (jnp.arange(atom_count * CAP)[:, None] == placement[None, :]).astype(jnp.int32)
     slots = jnp.arange(slot_count, dtype=jnp.int32)

time: 221 us -> 180 us (0.81)
  Pallas kernels: 208 us -> 173 us
  other arithmetic: 8.97 us -> 4.01 us
    pallas_call x2 -> x1, Pallas kernels: 208 us -> 173 us  [fused_call(): pl.pallas_call(functools.partial(fused_kernel, planes, auxes, step), out_...]
    convert_element_type x4 -> x0, other arithmetic: 2.85 us -> none  [the longest x1 1.28 us: per_device(): total = exchange_call(local_rows, fit_matrix.astype(jnp.float32))]
where the time goes in v1:
time: 180 us
  Pallas kernels  173 us (96%)
  other arithmetic  4.01 us (2%)
  local copies, waits for them, and re-layouts  2.38 us (1%)
    pallas_call x1, Pallas kernels, fused_call(): pl.pallas_call(functools.partial(fused_kernel, planes, auxes, step), out_...  173 us

profile of v1, /device:TPU:5, one launch (start us, length us, event | category | flops | bytes accessed | tf_op | source)
XLA Modules:
  0.0 180.1 jit_solution(4179259178283676811)
XLA Ops:
  0.7 0.7 broadcast_in_dim.9
  1.4 0.1 copy.14
  1.5 1.5 copy.13
  3.0 0.1 copy.15
  3.1 0.8 fusion.kron_ref
  3.9 173.0 %shard_map.82 = f32[512,1024]{1,0:T(8,128)} custom-call(s32[16]{0:T(128)} %bitcast.9, s32[16]{0:T(128)} %sub_ref.1, s32[16]{0:T(128)} %nu_ref.1, s32[1]{0:T(128)S(6)} %copy.16.live_ref, bf16[16,8,128,128]{3,2,1,0:T(8,128)(2,1)} %three_hbm.1, s32[128,8]{1,0:T(8,128)} %bitcast.6, bf16[4,128,128]{2,1,0:T(8,128)(2,1)} %bitcast.7, bf16[128,512]{1,0:T(8,128)(2,1)} %fusion.kron_ref), custom_call_target="tpu_custom_call" | custom-call | tf_op jit(solution)/shard_map/pallas_call | solution.py:1169
  176.9 3.2 %broadcast_multiply_fusion = f32[512,1024]{1,0:T(8,128)} fusion(f32[512,1024]{1,0:T(8,128)} %shard_map.82), kind=kLoop, calls=%fused_computation | loop fusion | flops 524288 | bytes 4194304 | tf_op jit(solution)/shard_map/mul | solution.py:1198
  (5 shorter events, 0.0 us)

commit v2 on v1

--- a/solution.py
+++ b/solution.py
@@ -533,7 +533,7 @@
 
 
 def fused_kernel(
-    planes, auxes, step,
+    planes, auxes, split,
     owner_ref, sub_ref, nu_ref, live_ref, three_hbm, mask_ref, coef_ref, kron_ref, out_ref,
     three, mexp, mrows, orb, order, nus, hits, hits_in, keep, xs, xr, up, dn, zb, own_rows, rows_all, fitted, kron, cs, cr,
     local_sem, orb_recv, orb_own, orb_line, orb_x, orb_core, code_sem, kron_send, kron_recv,
@@ -545,7 +545,8 @@
     rows, occ = per * size, coef_ref.shape[2]
     atoms = planes * 2
     half = per // 2
-    chunks = aux_here // step
+    chunks, part = aux_here * split, size // split
+    group = per * part
     shells = mask_ref.shape[1]
     shell = size // shells
     me = lax.axis_index("atom")
@@ -732,14 +733,9 @@
 
     def half_block(index, k):
         slot, nu = order[index], nus[index]
-        left = three[slot, pl.ds(k * step, step)] * mexp[slot][None, :, :]
-        value = jnp.dot(
-            left.reshape(step * size, size), orb[nu], preferred_element_type=jnp.float32
-        )
-        return value.reshape(step, size, occ).astype(jnp.bfloat16)
-
-    def span(k):
-        return pl.ds(k * step, step)
+        at = pl.ds(pl.multiple_of((k % split) * part, part), part)
+        left = three[slot, k // split, at, :] * mexp[slot, at, :]
+        return jnp.dot(left, orb[nu], preferred_element_type=jnp.float32).astype(jnp.bfloat16)
 
     def x_copy(k):
         return remote(xs.at[k], xr.at[k], x_send.at[k], x_recv.at[k], partner)
@@ -753,39 +749,28 @@
             [jnp.broadcast_to(hits_in[p * CAP + r, b:b + 1, :], (8, 128))[None] for r in range(CAP)]
             for b in range(per)
         ]
-        strip = 64
-
-        def strips(j, place, row):
-            at = pl.ds(pl.multiple_of(row * strip, strip), strip)
-            shape = (strip // 8, 8, occ)
-            own = [keep[k, p, r, j, at, :].astype(jnp.float32).reshape(shape) for r in range(CAP)]
-            other = [xr[k, p, r, j, at, :].astype(jnp.float32).reshape(shape) for r in range(CAP)]
-            for b in range(per):
-                to = pl.ds(pl.multiple_of(b * size + row * strip, strip), strip)
-                total = own[0] * own_hits[b][0] + other[0] * in_hits[b][0]
-                for r in range(1, CAP):
-                    total = total + own[r] * own_hits[b][r] + other[r] * in_hits[b][r]
-                for extra in extras:
-                    total = total + extra[p, place, to, :].astype(jnp.float32).reshape(shape)
-                value = total.reshape(strip, occ).astype(jnp.bfloat16)
-                if target is own_rows:
-                    target[place, to, :] = value
-                else:
-                    target[p, place, to, :] = value
-
-        for j in range(step):
-            place = k if step == 1 else k * step + j
-
-            @pl.loop(0, size // strip)
-            def _(row):
-                strips(j, place, row)
+        shape = (part // 8, 8, occ)
+        own = [keep[k, p, r].astype(jnp.float32).reshape(shape) for r in range(CAP)]
+        other = [xr[k, p, r].astype(jnp.float32).reshape(shape) for r in range(CAP)]
+        for b in range(per):
+            to = slice(b * part, (b + 1) * part)
+            total = own[0] * own_hits[b][0] + other[0] * in_hits[b][0]
+            for r in range(1, CAP):
+                total = total + own[r] * own_hits[b][r] + other[r] * in_hits[b][r]
+            for extra in extras:
+                total = total + extra[p, k, to, :].astype(jnp.float32).reshape(shape)
+            value = total.reshape(part, occ).astype(jnp.bfloat16)
+            if target is own_rows:
+                target[k, to, :] = value
+            else:
+                target[p, k, to, :] = value
 
     def up_copy(p, k):
-        ref = up.at[p, span(k)]
+        ref = up.at[p, k]
         return remote(ref, ref, up_send.at[p, k], up_recv.at[p, k], above)
 
     def dn_copy(p, k):
-        ref = dn.at[p, span(k)]
+        ref = dn.at[p, k]
         return remote(ref, ref, dn_send.at[p, k], dn_recv.at[p, k], below)
 
     def lane_of(p):
@@ -795,13 +780,13 @@
         return planes - 1 + (sender + auxes - target) % auxes
 
     def line_copy(src, p, k, send, device):
-        return remote(src, zb.at[lane_of(p), span(k)], send, line_recv.at[p, k], device)
+        return remote(src, zb.at[lane_of(p), k], send, line_recv.at[p, k], device)
 
     def b_copy(src, p, k):
-        return remote(src, zb.at[b_lane(ax, p), span(k)], b_send.at[p, k], b_recv.at[ax, k], at_aux(p))
+        return remote(src, zb.at[b_lane(ax, p), k], b_send.at[p, k], b_recv.at[ax, k], at_aux(p))
 
     def a_piece(column, u, k):
-        return rows_all.at[column, u, span(k)]
+        return rows_all.at[column, u, k]
 
     def a_copy(column, u, k, which, device):
         ref = a_piece(column, u, k)
@@ -809,11 +794,11 @@
 
     def own_a_copy(k, which, device):
         return remote(
-            own_rows.at[span(k)], a_piece(x, ax, k), a_send.at[which, k], a_recv.at[x, ax, k], device
+            own_rows.at[k], a_piece(x, ax, k), a_send.at[which, k], a_recv.at[x, ax, k], device
         )
 
     def own_copy(k):
-        return pltpu.make_async_copy(own_rows.at[span(k)], a_piece(x, ax, k), own_sem.at[k])
+        return pltpu.make_async_copy(own_rows.at[k], a_piece(x, ax, k), own_sem.at[k])
 
     def y_devices():
         return [((y + d) % ys) * 2 + c for d in range(1, ys)]
@@ -856,7 +841,7 @@
                 dn_copy(zz, kh).wait_recv()
                 extras.append(dn)
             add_dense(zz, kh, extras, own_rows)
-            mine = own_rows.at[span(kh)]
+            mine = own_rows.at[kh]
             own_copy(kh).start()
             if zz < planes - 1:
                 line_copy(mine, zz, kh, line_up.at[zz, kh], above).start()
@@ -872,7 +857,7 @@
 
         @pl.when(inside(kz))
         def _():
-            piece = zb.at[lane_of(p), span(kz)]
+            piece = zb.at[lane_of(p), kz]
             line_copy(piece, p, kz, line_up.at[p, kz], above).wait_recv()
             if p < zz < planes - 1:
                 line_copy(piece, p, kz, line_up.at[p, kz], above).start()
@@ -951,68 +936,70 @@
             for d in range(1, auxes):
                 u = (ax + d) % auxes
                 remote(
-                    zb.at[b_lane(u, ax), span(k)], zb.at[b_lane(u, ax), span(k)],
+                    zb.at[b_lane(u, ax), k], zb.at[b_lane(u, ax), k],
                     b_send.at[0, k], b_recv.at[u, k], core,
                 ).wait_recv()
 
     total_aux = auxes * aux_here
     strip = kron_ref.shape[0] // aux_here
+    pairs = [(u, p) for u in range(auxes) for p in range(aux_here)]
 
     def mix(load):
-        @pl.loop(0, rows // (2 * strip))
-        def _(j):
-            spots = [
-                pl.ds(pl.multiple_of(j * 2 * strip + h * strip, strip), strip) for h in range(2)
-            ]
-            right = jnp.concatenate(
-                [load(at).reshape(total_aux * strip, occ) for at in spots], axis=-1
-            )
-            value = jnp.dot(kron[...], right, preferred_element_type=jnp.float32).astype(jnp.bfloat16)
-            for h in range(2):
-                for q in range(total_aux):
-                    fitted[spots[h], q * occ:(q + 1) * occ] = value[
-                        q * strip:(q + 1) * strip, h * occ:(h + 1) * occ
-                    ]
+        for h in range(split):
+            @pl.loop(0, group // (2 * strip))
+            def _(j):
+                right = jnp.concatenate([
+                    jnp.concatenate([
+                        load(u, p * split + h, pl.ds(pl.multiple_of((2 * j + e) * strip, strip), strip))
+                        for u, p in pairs
+                    ], axis=0)
+                    for e in range(2)
+                ], axis=-1)
+                value = jnp.dot(kron[...], right, preferred_element_type=jnp.float32).astype(jnp.bfloat16)
+                for e in range(2):
+                    place = (2 * j + e) * strip
+                    to = (place // part) * size + h * part + place % part
+                    to = pl.ds(pl.multiple_of(to, strip), strip)
+                    for q in range(total_aux):
+                        fitted[to, q * occ:(q + 1) * occ] = value[
+                            q * strip:(q + 1) * strip, e * occ:(e + 1) * occ
+                        ]
 
     @pl.when(z == ax)
     def _():
-        mix(lambda at: rows_all[x, :, :, at, :])
+        mix(lambda u, k, at: rows_all[x, u, k, at, :])
 
     @pl.when(z != ax)
     def _():
-        mix(lambda at: jnp.concatenate([zb[b_lane(u, ax), :, at, :] for u in range(auxes)], axis=0))
-
-    block = 256
-
-    def product(column, j):
-        at = pl.ds(pl.multiple_of(j * block, block), block)
-        left = jnp.concatenate(
-            [rows_all[column, q // aux_here, q % aux_here, at, :] for q in range(total_aux)], axis=-1
-        )
-        return at, lax.dot_general(
+        mix(lambda u, k, at: zb[b_lane(u, ax), k, at, :])
+
+    def product(column, h):
+        left = jnp.concatenate([rows_all[column, u, p * split + h] for u, p in pairs], axis=-1)
+        return lax.dot_general(
             left, fitted[...], (((1,), (1,)), ((), ())), preferred_element_type=jnp.float32
         )
 
-    def c_copy(j):
-        at = pl.ds(pl.multiple_of(j * block, block), block)
-        return remote(cs.at[at], cr.at[at], c_send.at[j], c_recv.at[j], partner)
-
-    @pl.loop(0, rows // block)
-    def _(j):
-        at, value = product(1 - x, j)
-        cs[at, :] = value.astype(jnp.bfloat16)
-        c_copy(j).start()
-
-    @pl.loop(0, rows // block)
-    def _(j):
-        at, value = product(x, j)
-        out_ref[at, pl.ds(pl.multiple_of(x * rows, rows), rows)] = value
-
-    @pl.loop(0, rows // block)
-    def _(j):
-        c_copy(j).wait_recv()
-        at = pl.ds(pl.multiple_of(j * block, block), block)
-        out_ref[at, pl.ds(pl.multiple_of((1 - x) * rows, rows), rows)] = cr[at, :].astype(jnp.float32)
+    def c_copy(h):
+        return remote(cs.at[h], cr.at[h], c_send.at[h], c_recv.at[h], partner)
+
+    def place_rows(h, column, value):
+        for b in range(per):
+            to = pl.ds(pl.multiple_of(b * size + h * part, part), part)
+            out_ref[to, pl.ds(pl.multiple_of(column * rows, rows), rows)] = value[b * part:(b + 1) * part, :]
+
+    @pl.loop(0, split)
+    def _(h):
+        cs[h] = product(1 - x, h).astype(jnp.bfloat16)
+        c_copy(h).start()
+
+    @pl.loop(0, split)
+    def _(h):
+        place_rows(h, x, product(x, h))
+
+    @pl.loop(0, split)
+    def _(h):
+        c_copy(h).wait_recv()
+        place_rows(h, 1 - x, cr[h].astype(jnp.float32))
 
     @pl.when(has_up)
     def _():
@@ -1070,13 +1057,14 @@
             def _():
                 b_copy(a_piece(x, ax, k), p, k).wait_send()
 
-    @pl.loop(0, rows // block)
-    def _(j):
-        c_copy(j).wait_send()
-
-
-def fused_scratch(planes, auxes, step, slot_count, aux_here, size, occ, per, shells, kron_rows):
-    atoms, rows, chunks, ys = planes * 2, per * size, aux_here // step, auxes // 2
+    @pl.loop(0, split)
+    def _(h):
+        c_copy(h).wait_send()
+
+
+def fused_scratch(planes, auxes, split, slot_count, aux_here, size, occ, per, shells, kron_rows):
+    atoms, rows, chunks, ys = planes * 2, per * size, aux_here * split, auxes // 2
+    part, group = size // split, rows // split
     dma = pltpu.SemaphoreType.DMA
     half = jnp.bfloat16
     ways = 7 + 4 * (ys - 1)
@@ -1089,18 +1077,18 @@
         pltpu.SMEM((atoms * CAP,), jnp.int32),
         pltpu.VMEM((atoms * CAP, 8, 128), jnp.float32),
         pltpu.VMEM((planes * CAP, 8, 128), jnp.float32),
-        pltpu.VMEM((chunks, planes, CAP, step, size, occ), half),
-        pltpu.VMEM((chunks, planes, CAP, step, size, occ), half),
-        pltpu.VMEM((chunks, planes, CAP, step, size, occ), half),
-        pltpu.VMEM((planes, aux_here, rows, occ), half),
-        pltpu.VMEM((planes, aux_here, rows, occ), half),
-        pltpu.VMEM((planes + auxes - 1, aux_here, rows, occ), half),
-        pltpu.VMEM((aux_here, rows, occ), half),
-        pltpu.VMEM((2, auxes, aux_here, rows, occ), half),
+        pltpu.VMEM((chunks, planes, CAP, part, occ), half),
+        pltpu.VMEM((chunks, planes, CAP, part, occ), half),
+        pltpu.VMEM((chunks, planes, CAP, part, occ), half),
+        pltpu.VMEM((planes, chunks, group, occ), half),
+        pltpu.VMEM((planes, chunks, group, occ), half),
+        pltpu.VMEM((planes + auxes - 1, chunks, group, occ), half),
+        pltpu.VMEM((chunks, group, occ), half),
+        pltpu.VMEM((2, auxes, chunks, group, occ), half),
         pltpu.VMEM((rows, auxes * aux_here * occ), half),
         pltpu.VMEM((auxes * kron_rows, auxes * kron_rows), half),
-        pltpu.VMEM((rows, rows), half),
-        pltpu.VMEM((rows, rows), half),
+        pltpu.VMEM((split, group, rows), half),
+        pltpu.VMEM((split, group, rows), half),
     ]
     semaphores = [
         dma((3,)),
@@ -1126,36 +1114,35 @@
         dma((auxes, chunks)),
         dma((ways, chunks)),
         dma((2, auxes, chunks)),
-        dma((rows // 256,)),
-        dma((rows // 256,)),
+        dma((split,)),
+        dma((split,)),
     ]
     return buffers, semaphores
 
 
 VMEM_LIMIT = 60 * 1024 * 1024
 STRIP = 16
+SPLIT = 2
 
 
 def fused_plan(planes, auxes, three_index, pair_mask, coefficients):
     slot_count, aux_here, size, _ = three_index.shape
     rows, occ = coefficients.shape
     per, shells = rows // size, pair_mask.shape[1]
-    if planes != auxes or per % 2 or per > 8 or rows % 256 or shells % 8:
+    if planes != auxes or per % 2 or per > 8 or size % (32 * SPLIT) or shells % 8:
         return None
-    step = 1
     buffers, semaphores = fused_scratch(
-        planes, auxes, step, slot_count, aux_here, size, occ, per, shells, aux_here * STRIP
+        planes, auxes, SPLIT, slot_count, aux_here, size, occ, per, shells, aux_here * STRIP
     )
     held = rows * 2 * rows * 4 + 2 * rows * occ * 2
     for ref in buffers:
         held += math.prod(ref.shape) * jnp.dtype(ref.dtype).itemsize
     if held > VMEM_LIMIT - 4 * 1024 * 1024:
         return None
-    return step, buffers + semaphores
+    return buffers + semaphores
 
 
 def fused_call(plan, planes, auxes, three_index, pair_mask, owners, subs, nus, live, coefficients, fit_rows):
-    step, scratch = plan
     slot_count, aux_here, size, _ = three_index.shape
     rows, occ = coefficients.shape
     shells = pair_mask.shape[1]
@@ -1167,11 +1154,11 @@
     smem = pl.BlockSpec(memory_space=pltpu.SMEM)
     vmem = pl.BlockSpec(memory_space=pltpu.VMEM)
     return pl.pallas_call(
-        functools.partial(fused_kernel, planes, auxes, step),
+        functools.partial(fused_kernel, planes, auxes, SPLIT),
         out_shape=jax.ShapeDtypeStruct((rows, 2 * rows), jnp.float32),
         in_specs=[smem] * 4 + [pl.BlockSpec(memory_space=pl.ANY)] + [vmem] * 3,
         out_specs=vmem,
-        scratch_shapes=scratch,
+        scratch_shapes=plan,
         compiler_params=pltpu.CompilerParams(
             collective_id=2, has_side_effects=True, vmem_limit_bytes=VMEM_LIMIT
         ),

time: 180 us -> 171 us (0.950)
  Pallas kernels: 173 us -> 164 us
    pallas_call x1, Pallas kernels: 173 us -> 164 us  [fused_call(): pl.pallas_call(functools.partial(fused_kernel, planes, auxes, SPLIT), out...]
where the time goes in v2:
time: 171 us
  Pallas kernels  164 us (96%)
  other arithmetic  4.01 us (2%)
  local copies, waits for them, and re-layouts  2.38 us (1%)
    pallas_call x1, Pallas kernels, fused_call(): pl.pallas_call(functools.partial(fused_kernel, planes, auxes, SPLIT), out...  164 us

profile of v2, /device:TPU:5, one launch (start us, length us, event | category | flops | bytes accessed | tf_op | source)
XLA Modules:
  0.0 171.0 jit_solution(5551840975596879476)
XLA Ops:
  0.7 0.7 broadcast_in_dim.9
  1.4 0.1 copy.14
  1.5 1.5 copy.13
  3.0 0.1 copy.15
  3.1 0.8 fusion.kron_ref
  3.9 163.9 %shard_map.82 = f32[512,1024]{1,0:T(8,128)} custom-call(s32[16]{0:T(128)} %bitcast.9, s32[16]{0:T(128)} %sub_ref.1, s32[16]{0:T(128)} %nu_ref.1, s32[1]{0:T(128)S(6)} %copy.16.live_ref, bf16[16,8,128,128]{3,2,1,0:T(8,128)(2,1)} %three_hbm.1, s32[128,8]{1,0:T(8,128)} %bitcast.6, bf16[4,128,128]{2,1,0:T(8,128)(2,1)} %bitcast.7, bf16[128,512]{1,0:T(8,128)(2,1)} %fusion.kron_ref), custom_call_target="tpu_custom_call" | custom-call | tf_op jit(solution)/shard_map/pallas_call | solution.py:1156
  167.8 3.2 %broadcast_multiply_fusion = f32[512,1024]{1,0:T(8,128)} fusion(f32[512,1024]{1,0:T(8,128)} %shard_map.82), kind=kLoop, calls=%fused_computation | loop fusion | flops 524288 | bytes 4194304 | tf_op jit(solution)/shard_map/mul | solution.py:1185
  (5 shorter events, 0.0 us)

commit v3 on v2

--- a/solution.py
+++ b/solution.py
@@ -534,8 +534,8 @@
 
 def fused_kernel(
     planes, auxes, split,
-    owner_ref, sub_ref, nu_ref, live_ref, three_hbm, mask_ref, coef_ref, kron_ref, out_ref,
-    three, mexp, mrows, orb, order, nus, hits, hits_in, keep, xs, xr, up, dn, zb, own_rows, rows_all, fitted, kron, cs, cr,
+    owner_ref, sub_ref, nu_ref, live_ref, three_hbm, mask_ref, coef_ref, fit_ref, out_ref,
+    kron_ref, three, mexp, mrows, orb, order, nus, hits, hits_in, keep, xs, xr, up, dn, zb, own_rows, rows_all, fitted, kron, cs, cr,
     local_sem, orb_recv, orb_own, orb_line, orb_x, orb_core, code_sem, kron_send, kron_recv,
     x_send, x_recv, up_send, up_recv, dn_send, dn_recv,
     own_sem, line_up, line_dn, line_recv, b_send, b_recv, a_send, a_recv, c_send, c_recv,
@@ -581,10 +581,6 @@
 
     load_three = pltpu.make_async_copy(three_hbm, three, local_sem.at[0])
     load_three.start()
-    load_kron = pltpu.make_async_copy(
-        kron_ref, kron.at[pl.ds(pl.multiple_of(ax * kron_ref.shape[0], kron_ref.shape[0]), kron_ref.shape[0])], local_sem.at[1]
-    )
-    load_kron.start()
     load_orb = pltpu.make_async_copy(coef_ref, orb.at[pl.ds(me * per, per)], local_sem.at[2])
     load_orb.start()
 
@@ -654,20 +650,38 @@
     )
     send_codes.start()
 
+    def iota(shape, dim):
+        return lax.broadcasted_iota(jnp.int32, shape, dim)
+
+    aux_total = auxes * aux_here
+    strip = kron_ref.shape[0] // aux_here
+    tall, wide = kron_ref.shape
+    down = jnp.where(iota((tall, aux_here), 0) // strip == iota((tall, aux_here), 1), 1.0, 0.0)
+    along = jnp.where(iota((aux_total, wide), 1) // strip == iota((aux_total, wide), 0), 1.0, 0.0)
+    spread_rows = jnp.dot(down, fit_ref[...].astype(jnp.float32), preferred_element_type=jnp.float32)
+    spread_all = jnp.dot(spread_rows, along, preferred_element_type=jnp.float32)
+    same = iota((tall, wide), 0) % strip == iota((tall, wide), 1) % strip
+    kron_ref[...] = jnp.where(same, spread_all, 0.0).astype(jnp.bfloat16)
+    load_kron = pltpu.make_async_copy(
+        kron_ref, kron.at[pl.ds(pl.multiple_of(ax * kron_ref.shape[0], kron_ref.shape[0]), kron_ref.shape[0])], local_sem.at[1]
+    )
+    load_kron.start()
+
     spread = jnp.where(
         lax.broadcasted_iota(jnp.int32, (shells, size), 1) // shell
         == lax.broadcasted_iota(jnp.int32, (shells, size), 0), 1.0, 0.0
     )
-    mrows[...] = jnp.dot(
-        mask_ref[...].astype(jnp.float32), spread, preferred_element_type=jnp.float32
-    )
+    for m in range(shells):
+        mrows[m] = lax.dot_general(
+            mask_ref[m].astype(jnp.float32), spread, (((0,), (0,)), ((), ())),
+            preferred_element_type=jnp.float32,
+        )
 
     @pl.loop(0, slot_count)
     def _(s):
-        small = mrows[pl.ds(pl.multiple_of(s * shells, shells), shells), :]
-        for j in range(shells):
-            mexp[s, j * shell:(j + 1) * shell, :] = jnp.broadcast_to(
-                small[j:j + 1, :], (shell, size)
+        for m in range(shells):
+            mexp[s, m * shell:(m + 1) * shell, :] = jnp.broadcast_to(
+                mrows[m, pl.ds(s, 1), :], (shell, size)
             ).astype(jnp.bfloat16)
 
     def pass_orb(p, upward):
@@ -869,11 +883,6 @@
                 b_copy(piece, p, kz).start()
 
     def pass_rows(t, zz):
-        for d in range(1, planes):
-            for p in (zz - d, zz + d):
-                if 0 <= p < planes:
-                    pass_line(t, zz, p)
-
         ka = t - 2 - max(zz, planes - 1 - zz)
 
         @pl.when(inside(ka))
@@ -894,6 +903,11 @@
                 a_copy(1 - x, u, kb, 0, partner).wait_recv()
                 a_copy(1 - x, u, kb, 8 + 2 * (ys - 1) + 2 * n, core).start()
 
+        for d in range(1, planes):
+            for p in (zz - d, zz + d):
+                if 0 <= p < planes:
+                    pass_line(t, zz, p)
+
     @pl.loop(0, chunks + 2 * planes - 1)
     def _(t):
         @pl.when(t < chunks)
@@ -941,7 +955,6 @@
                 ).wait_recv()
 
     total_aux = auxes * aux_here
-    strip = kron_ref.shape[0] // aux_here
     pairs = [(u, p) for u in range(auxes) for p in range(aux_here)]
 
     def mix(load):
@@ -1069,9 +1082,10 @@
     half = jnp.bfloat16
     ways = 7 + 4 * (ys - 1)
     buffers = [
+        pltpu.VMEM((kron_rows, auxes * kron_rows), half),
         pltpu.VMEM((slot_count, aux_here, size, size), half),
         pltpu.VMEM((slot_count, size, size), half),
-        pltpu.VMEM((slot_count * shells, size), jnp.float32),
+        pltpu.VMEM((shells, slot_count, size), jnp.float32),
         pltpu.VMEM((atoms * per, size, occ), half),
         pltpu.SMEM((atoms * CAP,), jnp.int32),
         pltpu.SMEM((atoms * CAP,), jnp.int32),
@@ -1146,11 +1160,6 @@
     slot_count, aux_here, size, _ = three_index.shape
     rows, occ = coefficients.shape
     shells = pair_mask.shape[1]
-    total_aux = fit_rows.shape[1]
-    width = jnp.repeat(jnp.repeat(fit_rows, STRIP, 0), STRIP, 1)
-    row = lax.broadcasted_iota(jnp.int32, width.shape, 0) % STRIP
-    col = lax.broadcasted_iota(jnp.int32, width.shape, 1) % STRIP
-    kron_rows = jnp.where(row == col, width, jnp.zeros_like(width))
     smem = pl.BlockSpec(memory_space=pltpu.SMEM)
     vmem = pl.BlockSpec(memory_space=pltpu.VMEM)
     return pl.pallas_call(
@@ -1163,8 +1172,8 @@
             collective_id=2, has_side_effects=True, vmem_limit_bytes=VMEM_LIMIT
         ),
     )(
-        owners, subs, nus, live, three_index, pair_mask.reshape(slot_count * shells, shells),
-        coefficients.reshape(rows // size, size, occ), kron_rows,
+        owners, subs, nus, live, three_index, pair_mask.transpose(1, 2, 0),
+        coefficients.reshape(rows // size, size, occ), fit_rows,
     )
 
 

time: 171 us -> 165 us (0.965)
  Pallas kernels: 164 us -> 161 us
  local copies, waits for them, and re-layouts: 2.38 us -> 0 us
    pallas_call x1, Pallas kernels: 164 us -> 161 us  [fused_call(): pl.pallas_call(functools.partial(fused_kernel, planes, auxes, SPLIT), out...]
where the time goes in v3:
time: 165 us
  Pallas kernels  161 us (98%)
  other arithmetic  3.22 us (2%)
    pallas_call x1, Pallas kernels, fused_call(): pl.pallas_call(functools.partial(fused_kernel, planes, auxes, SPLIT), out...  161 us

profile of v3, /device:TPU:5, one launch (start us, length us, event | category | flops | bytes accessed | tf_op | source)
XLA Modules:
  0.0 164.5 jit_solution(13981275573065961468)
XLA Ops:
  0.7 160.7 %shard_map.82 = f32[512,1024]{1,0:T(8,128)} custom-call(s32[16]{0:T(128)} %bitcast.5, s32[16]{0:T(128)} %sub_ref.1, s32[16]{0:T(128)} %nu_ref.1, s32[1]{0:T(128)S(6)} %copy.9.live_ref, bf16[16,8,128,128]{3,2,1,0:T(8,128)(2,1)} %three_hbm.1, s32[8,8,16]{2,1,0:T(8,128)} %bitcast.4, bf16[4,128,128]{2,1,0:T(8,128)(2,1)} %bitcast.3, bf16[8,32]{1,0:T(8,128)(2,1)} %fit_ref.1), custom_call_target="tpu_custom_call" | custom-call | tf_op jit(solution)/shard_map/pallas_call | solution.py:1165
  161.3 3.2 %broadcast_multiply_fusion = f32[512,1024]{1,0:T(8,128)} fusion(f32[512,1024]{1,0:T(8,128)} %shard_map.82), kind=kLoop, calls=%fused_computation | loop fusion | flops 524288 | bytes 4194304 | tf_op jit(solution)/shard_map/mul | solution.py:1194

commit v4 on v3

--- a/solution.py
+++ b/solution.py
@@ -957,9 +957,12 @@
     total_aux = auxes * aux_here
     pairs = [(u, p) for u in range(auxes) for p in range(aux_here)]
 
-    def mix(load):
+    halves = 2
+    turns = group // (2 * strip) // halves
+
+    def mix(load, v):
         for h in range(split):
-            @pl.loop(0, group // (2 * strip))
+            @pl.loop(v * turns, (v + 1) * turns)
             def _(j):
                 right = jnp.concatenate([
                     jnp.concatenate([
@@ -978,41 +981,51 @@
                             q * strip:(q + 1) * strip, e * occ:(e + 1) * occ
                         ]
 
-    @pl.when(z == ax)
-    def _():
-        mix(lambda u, k, at: rows_all[x, u, k, at, :])
-
-    @pl.when(z != ax)
-    def _():
-        mix(lambda u, k, at: zb[b_lane(u, ax), k, at, :])
-
-    def product(column, h):
+    def mix_half(v):
+        @pl.when(z == ax)
+        def _():
+            mix(lambda u, k, at: rows_all[x, u, k, at, :], v)
+
+        @pl.when(z != ax)
+        def _():
+            mix(lambda u, k, at: zb[b_lane(u, ax), k, at, :], v)
+
+    width = rows // halves
+
+    def product(column, h, v):
         left = jnp.concatenate([rows_all[column, u, p * split + h] for u, p in pairs], axis=-1)
         return lax.dot_general(
-            left, fitted[...], (((1,), (1,)), ((), ())), preferred_element_type=jnp.float32
+            left, fitted[v * width:(v + 1) * width, :], (((1,), (1,)), ((), ())),
+            preferred_element_type=jnp.float32,
         )
 
-    def c_copy(h):
-        return remote(cs.at[h], cr.at[h], c_send.at[h], c_recv.at[h], partner)
-
-    def place_rows(h, column, value):
+    def c_copy(h, v):
+        return remote(cs.at[v, h], cr.at[v, h], c_send.at[v, h], c_recv.at[v, h], partner)
+
+    def place_rows(h, v, column, value):
         for b in range(per):
             to = pl.ds(pl.multiple_of(b * size + h * part, part), part)
-            out_ref[to, pl.ds(pl.multiple_of(column * rows, rows), rows)] = value[b * part:(b + 1) * part, :]
-
-    @pl.loop(0, split)
-    def _(h):
-        cs[h] = product(1 - x, h).astype(jnp.bfloat16)
-        c_copy(h).start()
-
-    @pl.loop(0, split)
-    def _(h):
-        place_rows(h, x, product(x, h))
-
-    @pl.loop(0, split)
-    def _(h):
-        c_copy(h).wait_recv()
-        place_rows(h, 1 - x, cr[h].astype(jnp.float32))
+            cols = pl.ds(pl.multiple_of(column * rows + v * width, width), width)
+            out_ref[to, cols] = value[b * part:(b + 1) * part, :]
+
+    for v in range(halves):
+        mix_half(v)
+
+        @pl.loop(0, split)
+        def _(h):
+            cs[v, h] = product(1 - x, h, v).astype(jnp.bfloat16)
+            c_copy(h, v).start()
+
+    for v in range(halves):
+        @pl.loop(0, split)
+        def _(h):
+            place_rows(h, v, x, product(x, h, v))
+
+    for v in range(halves):
+        @pl.loop(0, split)
+        def _(h):
+            c_copy(h, v).wait_recv()
+            place_rows(h, v, 1 - x, cr[v, h].astype(jnp.float32))
 
     @pl.when(has_up)
     def _():
@@ -1072,7 +1085,8 @@
 
     @pl.loop(0, split)
     def _(h):
-        c_copy(h).wait_send()
+        for v in range(halves):
+            c_copy(h, v).wait_send()
 
 
 def fused_scratch(planes, auxes, split, slot_count, aux_here, size, occ, per, shells, kron_rows):
@@ -1101,8 +1115,8 @@
         pltpu.VMEM((2, auxes, chunks, group, occ), half),
         pltpu.VMEM((rows, auxes * aux_here * occ), half),
         pltpu.VMEM((auxes * kron_rows, auxes * kron_rows), half),
-        pltpu.VMEM((split, group, rows), half),
-        pltpu.VMEM((split, group, rows), half),
+        pltpu.VMEM((2, split, group, rows // 2), half),
+        pltpu.VMEM((2, split, group, rows // 2), half),
     ]
     semaphores = [
         dma((3,)),
@@ -1128,8 +1142,8 @@
         dma((auxes, chunks)),
         dma((ways, chunks)),
         dma((2, auxes, chunks)),
-        dma((split,)),
-        dma((split,)),
+        dma((2, split)),
+        dma((2, split)),
     ]
     return buffers, semaphores
 
@@ -1143,7 +1157,7 @@
     slot_count, aux_here, size, _ = three_index.shape
     rows, occ = coefficients.shape
     per, shells = rows // size, pair_mask.shape[1]
-    if planes != auxes or per % 2 or per > 8 or size % (32 * SPLIT) or shells % 8:
+    if planes != auxes or per % 2 or per > 8 or size % (32 * SPLIT) or shells % 8 or rows % (2 * 128):
         return None
     buffers, semaphores = fused_scratch(
         planes, auxes, SPLIT, slot_count, aux_here, size, occ, per, shells, aux_here * STRIP

time: 165 us -> 162 us (0.982)
  Pallas kernels: 161 us -> 158 us
    pallas_call x1, Pallas kernels: 161 us -> 158 us  [fused_call(): pl.pallas_call(functools.partial(fused_kernel, planes, auxes, SPLIT), out...]
where the time goes in v4:
time: 162 us; the launch traced here: 161 us
  Pallas kernels  158 us (98%)
  other arithmetic  3.22 us (2%)
    pallas_call x1, Pallas kernels, fused_call(): pl.pallas_call(functools.partial(fused_kernel, planes, auxes, SPLIT), out...  158 us

profile of v4, /device:TPU:5, one launch (start us, length us, event | category | flops | bytes accessed | tf_op | source)
XLA Modules:
  0.0 161.4 jit_solution(5526346051678026792)
XLA Ops:
  0.7 157.6 %shard_map.82 = f32[512,1024]{1,0:T(8,128)} custom-call(s32[16]{0:T(128)} %bitcast.5, s32[16]{0:T(128)} %sub_ref.1, s32[16]{0:T(128)} %nu_ref.1, s32[1]{0:T(128)S(6)} %copy.9.live_ref, bf16[16,8,128,128]{3,2,1,0:T(8,128)(2,1)} %three_hbm.1, s32[8,8,16]{2,1,0:T(8,128)} %bitcast.4, bf16[4,128,128]{2,1,0:T(8,128)(2,1)} %bitcast.3, bf16[8,32]{1,0:T(8,128)(2,1)} %fit_ref.1), custom_call_target="tpu_custom_call" | custom-call | tf_op jit(solution)/shard_map/pallas_call | solution.py:1179
  158.2 3.2 %broadcast_multiply_fusion = f32[512,1024]{1,0:T(8,128)} fusion(f32[512,1024]{1,0:T(8,128)} %shard_map.82), kind=kLoop, calls=%fused_computation | loop fusion | flops 524288 | bytes 4194304 | tf_op jit(solution)/shard_map/mul | solution.py:1208
